TPU v7x, 32 devices: a whole 2x2x4 slice. The times are simulated.
32 devices in a mesh: fsdp: 16 (over z, x, core), dp: 2 (over y).
Axes of the slice: x: 2, y: 2, z: 4, core: 2. Of those that a mesh axis runs over, the one named last changes fastest.
Arguments:
- tokens: bfloat16 [32768, 768], P(('fsdp', 'dp')), may hold values from -6 to 6
- segment_ids: int32 [32, 1024], P(('fsdp', 'dp')), may hold values from -1 to 15, as said below
- projection: float32 [12, 32, 64], replicated, may hold values from -0.75 to 0.75
- norm1_gain: bfloat16 [768], P('fsdp'), may hold values from 0.5 to 1.5
- norm1_bias: bfloat16 [768], P('fsdp'), may hold values from -1.1953125 to 1.1953125
- qkv_weight: bfloat16 [768, 2304], P('fsdp'), may hold values from -0.21875 to 0.21875
- qkv_bias: bfloat16 [2304], P('fsdp'), may hold values from -1.1953125 to 1.1953125
- out_weight: bfloat16 [768, 768], P('fsdp'), may hold values from -1.5 to 1.5
- out_bias: bfloat16 [768], P('fsdp'), may hold values from -1.1953125 to 1.1953125
- norm2_gain: bfloat16 [768], P('fsdp'), may hold values from 0.5 to 1.5
- norm2_bias: bfloat16 [768], P('fsdp'), may hold values from -1.1953125 to 1.1953125
- in_weight: bfloat16 [768, 3072], P('fsdp'), may hold values from -0.21875 to 0.21875
- in_bias: bfloat16 [3072], P('fsdp'), may hold values from -1.1953125 to 1.1953125
- ffn_out_weight: bfloat16 [3072, 768], P('fsdp'), may hold values from -0.109375 to 0.109375
- ffn_out_bias: bfloat16 [768], P('fsdp'), may hold values from -1.1953125 to 1.1953125
- cotangent: bfloat16 [32768, 768], P(('fsdp', 'dp')), may hold values from -6 to 6
Outputs:
- output: bfloat16 [32768, 768], P(('fsdp', 'dp'))
- tokens_grad: bfloat16 [32768, 768], P(('fsdp', 'dp'))
- norm1_gain_grad: float32 [768], P('fsdp')
- norm1_bias_grad: float32 [768], P('fsdp')
- qkv_weight_grad: float32 [768, 2304], P('fsdp')
- query_key_bias_grad: float32 [1536], P('fsdp')
- value_bias_grad: float32 [768], P('fsdp')
- out_weight_grad: float32 [768, 768], P('fsdp')
- out_bias_grad: float32 [768], P('fsdp')
- norm2_gain_grad: float32 [768], P('fsdp')
- norm2_bias_grad: float32 [768], P('fsdp')
- in_weight_grad: float32 [768, 3072], P('fsdp')
- in_bias_grad: float32 [3072], P('fsdp')
- ffn_out_weight_grad: float32 [3072, 768], P('fsdp')
- ffn_out_bias_grad: float32 [768], P('fsdp')
Inputs may be any that keep to these rules, and one draw needn't show every extreme that they name: `segment_ids`: in each sequence the ids never fall until the padding; the last 1 to 256 rows of every sequence are -1 and no others; every sequence reaches id 16 - 1; some segments may have no rows.
All inputs are finite; a program needn't handle non-finite values.
Results may differ from a plain program's by a relative error of at most 0.01.
Values may be sent and summed in bfloat16 or wider, within the bound.
A program may use at most 192 MiB of HBM per device.

v0:
```python
import jax
import jax.numpy as jnp
from jax import lax
from jax.sharding import PartitionSpec as P

HEADS = 12
HEAD_DIM = 64
SEGS = 16
highest = lax.Precision.HIGHEST
epsilon = 1e-05


def norm_forward(rows, gain, shift):
    row_mean = jnp.mean(rows, axis=-1, keepdims=True)
    centred = rows - row_mean
    inv_std = lax.rsqrt(jnp.mean(centred * centred, axis=-1, keepdims=True) + epsilon)
    normed = centred * inv_std
    return (normed * gain + shift, normed, inv_std)


def norm_backward(incoming, normed, inv_std, gain):
    scaled = incoming * gain
    mean_one = jnp.mean(scaled, axis=-1, keepdims=True)
    mean_two = jnp.mean(scaled * normed, axis=-1, keepdims=True)
    input_grad = inv_std * (scaled - mean_one - normed * mean_two)
    return (input_grad, jnp.sum(incoming * normed, axis=0), jnp.sum(incoming, axis=0))


def rotary_tables(length, half_width):
    positions = jnp.arange(length, dtype=jnp.float32)
    frequency = 10000.0 ** (-jnp.arange(half_width, dtype=jnp.float32) / half_width)
    angles = positions[:, None] * frequency[None, :]
    return (jnp.cos(angles)[:, None, :], jnp.sin(angles)[:, None, :])


def rotate(values, cosine, sine):
    half_width = values.shape[-1] // 2
    lower_half = values[..., :half_width]
    upper_half = values[..., half_width:]
    return jnp.concatenate(
        [lower_half * cosine - upper_half * sine, lower_half * sine + upper_half * cosine], axis=-1
    )


def segment_core(query_rows, key_rows, value_rows, segment, projection):
    length = query_rows.shape[0]
    cosine, sine = rotary_tables(length, query_rows.shape[-1] // 2)
    feat_query = jax.nn.softplus(
        jnp.einsum("nhd,hfd->nhf", rotate(query_rows, cosine, sine), projection, precision=highest)
    )
    feat_key = jax.nn.softplus(
        jnp.einsum("nhd,hfd->nhf", rotate(key_rows, cosine, sine), projection, precision=highest)
    )
    member = (segment[:, None] == jnp.arange(SEGS, dtype=jnp.int32)[None, :]).astype(jnp.float32)
    present = jnp.sum(member, axis=-1)
    masked_keys = member[:, :, None, None] * feat_key[:, None]
    kv_state = jnp.einsum("nshf,nhd->shfd", masked_keys, value_rows, precision=highest)
    totals = jnp.sum(masked_keys, axis=0)
    masked_queries = member[:, :, None, None] * feat_query[:, None]
    numerator = jnp.einsum("nshf,shfd->nhd", masked_queries, kv_state, precision=highest)
    denominator = (
        jnp.einsum("nshf,shf->nh", masked_queries, totals, precision=highest)
        + (1.0 - present)[:, None]
    )
    return numerator / denominator[:, :, None]


def attend(projected, segment_ids, projection):
    seq_count, length = segment_ids.shape
    shaped = projected.reshape(seq_count, length, 3, HEADS, HEAD_DIM)

    def one_sequence(pieces):
        rows, segment = pieces
        return segment_core(rows[:, 0], rows[:, 1], rows[:, 2], segment, projection)

    return lax.map(one_sequence, (shaped, segment_ids)).reshape(
        seq_count * length, HEADS * HEAD_DIM
    )


def attend_back(projected, segment_ids, projection, grad_attended):
    seq_count, length = segment_ids.shape
    shaped = projected.reshape(seq_count, length, 3, HEADS, HEAD_DIM)
    upstream_rows = grad_attended.reshape(seq_count, length, HEADS, HEAD_DIM)

    def one_sequence(pieces):
        rows, segment, upstream = pieces

        def local_core(query_rows, key_rows, value_rows):
            return segment_core(query_rows, key_rows, value_rows, segment, projection)

        unused, pull = jax.vjp(local_core, rows[:, 0], rows[:, 1], rows[:, 2])
        grads = pull(upstream)
        return jnp.stack(grads, axis=1)

    result = lax.map(one_sequence, (shaped, segment_ids, upstream_rows))
    return result.reshape(seq_count * length, 3 * HEADS * HEAD_DIM)


def contract_rows(left, right):
    return lax.dot_general(
        left, right, (((0,), (0,)), ((), ())), preferred_element_type=jnp.float32
    )


def contract_cols(left, right):
    return lax.dot_general(
        left, right, (((1,), (1,)), ((), ())), preferred_element_type=jnp.float32
    )


def fetch_block(params):
    return (
        lax.all_gather(params[0], "fsdp", axis=0, tiled=True),
        lax.all_gather(params[1], "fsdp", axis=0, tiled=True),
        lax.all_gather(params[2], "fsdp", axis=0, tiled=True),
        lax.all_gather(params[3], "fsdp", axis=0, tiled=True),
        lax.all_gather(params[4], "fsdp", axis=0, tiled=True),
        lax.all_gather(params[5], "fsdp", axis=0, tiled=True),
    )


def backward_weights(params):
    return (
        lax.all_gather(params[0], "fsdp", axis=0, tiled=True),
        lax.all_gather(params[1], "fsdp", axis=0, tiled=True),
        lax.all_gather(params[2], "fsdp", axis=0, tiled=True),
        lax.all_gather(params[3], "fsdp", axis=0, tiled=True),
        lax.all_gather(params[4], "fsdp", axis=0, tiled=True),
        lax.all_gather(params[5], "fsdp", axis=0, tiled=True),
    )


def reduce_grads(grads):
    pieces = (
        lax.psum_scatter(grads[0], "fsdp", scatter_dimension=0, tiled=True),
        lax.psum_scatter(grads[1], "fsdp", scatter_dimension=0, tiled=True),
        lax.psum_scatter(grads[2], "fsdp", scatter_dimension=0, tiled=True),
        lax.psum_scatter(grads[3], "fsdp", scatter_dimension=0, tiled=True),
        lax.psum_scatter(grads[4], "fsdp", scatter_dimension=0, tiled=True),
        lax.psum_scatter(grads[5], "fsdp", scatter_dimension=0, tiled=True),
    )
    return (
        lax.psum(pieces[0].astype(jnp.bfloat16), "dp").astype(jnp.float32),
        lax.psum(pieces[1].astype(jnp.bfloat16), "dp").astype(jnp.float32),
        lax.psum(pieces[2].astype(jnp.bfloat16), "dp").astype(jnp.float32),
        lax.psum(pieces[3].astype(jnp.bfloat16), "dp").astype(jnp.float32),
        lax.psum(pieces[4].astype(jnp.bfloat16), "dp").astype(jnp.float32),
        lax.psum(pieces[5].astype(jnp.bfloat16), "dp").astype(jnp.float32),
    )


def body(
    tokens,
    segment_ids,
    projection,
    norm1_gain,
    norm1_bias,
    qkv_weight,
    qkv_bias,
    out_weight,
    out_bias,
    norm2_gain,
    norm2_bias,
    in_weight,
    in_bias,
    ffn_out_weight,
    ffn_out_bias,
    cotangent,
):
    attn_local = (norm1_gain, norm1_bias, qkv_weight, qkv_bias, out_weight, out_bias)
    ffn_local = (norm2_gain, norm2_bias, in_weight, in_bias, ffn_out_weight, ffn_out_bias)
    model_width = tokens.shape[1]
    groups = lax.axis_size("fsdp")
    attn_full = fetch_block(attn_local)
    gain_one, shift_one, weight_qkv, bias_qkv, weight_out, bias_out = attn_full
    residual = tokens.astype(jnp.float32)
    normed_out_one, normed_one, inv_one = norm_forward(
        residual, gain_one.astype(jnp.float32), shift_one.astype(jnp.float32)
    )
    hidden_one = normed_out_one.astype(jnp.bfloat16)
    projected = jnp.dot(
        hidden_one, weight_qkv, preferred_element_type=jnp.float32
    ) + bias_qkv.astype(jnp.float32)
    attended = attend(projected, segment_ids, projection).astype(jnp.bfloat16)
    branch_one = jnp.dot(
        attended, weight_out, preferred_element_type=jnp.float32
    ) + bias_out.astype(jnp.float32)
    middle = residual + branch_one
    ffn_full = fetch_block(ffn_local)
    gain_two, shift_two, weight_in, bias_in, weight_ffo, bias_ffo = ffn_full
    normed_out_two, normed_two, inv_two = norm_forward(
        middle, gain_two.astype(jnp.float32), shift_two.astype(jnp.float32)
    )
    hidden_two = normed_out_two.astype(jnp.bfloat16)
    pre_act = jnp.dot(hidden_two, weight_in, preferred_element_type=jnp.float32) + bias_in.astype(
        jnp.float32
    )
    activated = jax.nn.gelu(pre_act, approximate=False).astype(jnp.bfloat16)
    branch_two = jnp.dot(
        activated, weight_ffo, preferred_element_type=jnp.float32
    ) + bias_ffo.astype(jnp.float32)
    output = (middle + branch_two).astype(jnp.bfloat16)
    upstream = cotangent.astype(jnp.float32)
    ffn_back = backward_weights(ffn_local)
    back_gain_two, unused_shift_two, back_in, unused_bias_in, back_ffo, unused_bias_ffo = ffn_back
    grad_ffo_weight = contract_rows(activated, cotangent)
    grad_ffo_bias = jnp.sum(upstream, axis=0)
    grad_activated = contract_cols(cotangent, back_ffo)
    slope = (
        0.5 * (1.0 + lax.erf(pre_act * 0.7071067811865476))
        + pre_act * jnp.exp(-0.5 * pre_act * pre_act) * 0.3989422804014327
    )
    grad_pre = (grad_activated * slope).astype(jnp.bfloat16)
    grad_in_weight = contract_rows(hidden_two, grad_pre)
    grad_in_bias = jnp.sum(grad_pre.astype(jnp.float32), axis=0)
    grad_hidden_two = contract_cols(grad_pre, back_in)
    back_two, grad_gain_two, grad_shift_two = norm_backward(
        grad_hidden_two, normed_two, inv_two, back_gain_two.astype(jnp.float32)
    )
    grad_middle = upstream + back_two
    ffn_grads = reduce_grads(
        (
            grad_gain_two,
            grad_shift_two,
            grad_in_weight,
            grad_in_bias,
            grad_ffo_weight,
            grad_ffo_bias,
        )
    )
    attn_back = backward_weights(attn_local)
    back_gain_one, unused_shift_one, back_qkv, unused_bias_qkv, back_out, unused_bias_out = (
        attn_back
    )
    grad_branch = grad_middle.astype(jnp.bfloat16)
    grad_out_weight = contract_rows(attended, grad_branch)
    grad_out_bias = jnp.sum(grad_branch.astype(jnp.float32), axis=0)
    grad_attended = contract_cols(grad_branch, back_out)
    grad_projected = attend_back(projected, segment_ids, projection, grad_attended).astype(
        jnp.bfloat16
    )
    grad_qkv_weight = contract_rows(hidden_one, grad_projected)
    grad_qkv_bias = jnp.sum(grad_projected.astype(jnp.float32), axis=0)
    bias_packed = jnp.concatenate(
        [
            grad_qkv_bias[: 2 * model_width].reshape(groups, -1),
            grad_qkv_bias[2 * model_width :].reshape(groups, -1),
        ],
        axis=1,
    ).reshape(-1)
    grad_hidden_one = contract_cols(grad_projected, back_qkv)
    back_one, grad_gain_one, grad_shift_one = norm_backward(
        grad_hidden_one, normed_one, inv_one, back_gain_one.astype(jnp.float32)
    )
    tokens_grad = (grad_middle + back_one).astype(jnp.bfloat16)
    attn_grads = reduce_grads(
        (
            grad_gain_one,
            grad_shift_one,
            grad_qkv_weight,
            bias_packed,
            grad_out_weight,
            grad_out_bias,
        )
    )
    owned_bias = attn_grads[3]
    split_point = 2 * model_width // groups
    return (
        output,
        tokens_grad,
        attn_grads[0],
        attn_grads[1],
        attn_grads[2],
        owned_bias[:split_point],
        owned_bias[split_point:],
        attn_grads[4],
        attn_grads[5],
        ffn_grads[0],
        ffn_grads[1],
        ffn_grads[2],
        ffn_grads[3],
        ffn_grads[4],
        ffn_grads[5],
    )


def solution(mesh):
    in_specs = (
        P(("fsdp", "dp"), None),
        P(("fsdp", "dp"), None),
        P(),
        P("fsdp"),
        P("fsdp"),
        P("fsdp", None),
        P("fsdp"),
        P("fsdp", None),
        P("fsdp"),
        P("fsdp"),
        P("fsdp"),
        P("fsdp", None),
        P("fsdp"),
        P("fsdp", None),
        P("fsdp"),
        P(("fsdp", "dp"), None),
    )
    out_specs = (
        P(("fsdp", "dp"), None),
        P(("fsdp", "dp"), None),
        P("fsdp"),
        P("fsdp"),
        P("fsdp", None),
        P("fsdp"),
        P("fsdp"),
        P("fsdp", None),
        P("fsdp"),
        P("fsdp"),
        P("fsdp"),
        P("fsdp", None),
        P("fsdp"),
        P("fsdp", None),
        P("fsdp"),
    )
    return jax.shard_map(body, mesh=mesh, in_specs=in_specs, out_specs=out_specs, check_vma=False)
```

profile of v0, /device:TPU:0, one launch (start us, length us, event | category | flops | bytes accessed | tf_op | source)
XLA Modules:
  0.0 792.6 jit_solution(11601006534894251956)
XLA Ops:
  22.0 63.5 %all-reduce.21 = (bf16[2304]{0:T(1024)(128)(2,1)S(1)}, bf16[768]{0:T(1024)(128)(2,1)S(1)}, bf16[768]{0:T(1024)(128)(2,1)S(1)}, bf16[768]{0:T(1024)(128)(2,1)}, b...) all-reduce(bf16[2304]{0:T(1024)(128)(2,1)S(1)} %dynamic-update-slic, ...), channel_id=1, replica_groups=mesh['fsdp'=16,'dp'=2] {'fsdp'}, use_global_device_ids=true, to_apply=%add.6 | all-reduce | flops 9984 | bytes 39936
  94.6 8.6 %convolution_add_fusion = f32[1024,2304]{1,0:T(8,128)} fusion(bf16[768,2304]{1,0:T(8,128)(2,1)} %all-gather.5.cloned.1.call-done, f32[2304]{0:T(1024)} %convert_element_type.162, bf16[1024,768]{0,1:T(8,128)(2,1)S(1)} %copy.55, f32[768]{0:T(1024)} %convert_element_type.160, f32[768]{0:T(1024)S(1)} %convert_element_type.159, f32[1024]{0:T(1024)S(1)} %add_rsqrt_fusion.1, ...), kind=kOutput, calls=%fused_computation.58 | convolution fusion | flops 3630956544 | bytes 14572544 | tf_op jit(solution)/shard_map/dot_general | solution.py:182
  103.3 9.7 %copy.56 = f32[1024,2304]{0,1:T(8,128)} copy(f32[1024,2304]{1,0:T(8,128)} %convolution_add_fusion) | data formatting | bytes 18874368 | tf_op jit(solution)/shard_map/add | solution.py:182
  113.0 3.8 slice_bitcast_fusion.1
  118.4 3.7 compare_select_fusion.5
  122.1 21.6 %fusion.10 = f32[12,64,16,32]{1,3,2,0:T(8,128)S(1)} fusion(f32[1024,12,32]{0,2,1:T(8,128)S(1)} %get-tuple-element.162, f32[1024,16]{0,1:T(8,128)S(1)} %fusion.102, f32[1024,3,12,64]{0,3,2,1:T(8,128)S(1)} %bitcast.184), kind=kOutput, calls=%fused_computation.11 | convolution fusion | flops 4838129664 | bytes 6356992 | tf_op jit(solution)/shard_map/while/body/eval_jaxpr/nshf,nhd->shfd/dot_general | solution.py:57
  145.6 3.7 compare_select_fusion.4
  149.3 16.0 %fusion.4 = f32[12,1,1024,1]{2,1,3,0:T(1,128)S(1)} fusion(f32[16,12,32,1]{2,3,0,1:T(1,128)S(1)} %bitcast.190, f32[1024,12,32]{0,2,1:T(8,128)S(1)} %get-tuple-element.160, f32[1024,16]{0,1:T(8,128)S(1)} %fusion.102), kind=kOutput, calls=%fused_computation.4 | convolution fusion | flops 81788928 | bytes 1712128 | tf_op jit(solution)/shard_map/while/body/eval_jaxpr/nshf,shf->nh/dot_general | solution.py:62
  166.0 18.3 %fusion.65 = (bf16[1024,12,64]{0,2,1:T(8,128)(2,1)}, f32[12,64,1024,1]{2,1,3,0:T(8,128)}) fusion(f32[1024,12]{0,1:T(8,128)S(1)} %fusion.101, f32[1024,12,32]{0,2,1:T(8,128)S(1)} %get-tuple-element.160, f32[1024,16]{0,1:T(8,128)S(1)} %fusion.102, f32[12,64,16,32]{1,3,2,0:T(8,128)S(1)} %fusion.10), kind=kOutput, calls=%fused_computation.98 | convolution fusion | flops 4839702528 | bytes 7979008 | tf_op jit(solution)/shard_map/while/body/eval_jaxpr/nshf,shfd->nhd/dot_general | solution.py:60
  189.9 38.9 %fusion.16 = (bf16[1024,3072]{1,0:T(8,128)(2,1)}, f32[1024,3072]{1,0:T(8,128)}) fusion(f32[3072]{0:T(1024)S(1)} %copy-done.34, bf16[768,3072]{1,0:T(8,128)(2,1)} %all-gather.9.cloned.1.call-done, f32[1024,768]{0,1:T(8,128)} %copy-done.3, f32[768]{0:T(1024)S(1)} %copy-done.37, f32[768]{0:T(1024)S(1)} %convert_element_type.167, f32[1024]{0:T(1024)S(1)} %add_rsqrt_fusion, ...), kind=kOutput, calls=%fused_computation.21 | convolution fusion | flops 5043388416 | bytes 26765312 | tf_op jit(solution)/shard_map/dot_general | solution.py:196
  228.8 11.9 %convert_reduce_fusion = (f32[3072]{0:T(1024)S(1)}, bf16[1024,3072]{1,0:T(8,128)(2,1)S(1)}) fusion(f32[1024,3072]{1,0:T(8,128)} %get-tuple-element.169, f32[3072]{0:T(1024)S(1)} %copy-done.34, bf16[1024,768]{1,0:T(8,128)(2,1)S(1)} %copy-done.12, bf16[3072,768]{1,0:T(8,128)(2,1)} %all-gather.11.cloned.1.call-done), kind=kOutput, calls=%fused_computation.28 | convolution fusion | flops 4872729600 | bytes 25190400 | tf_op jit(solution)/shard_map/dot_general | solution.py:107
  240.8 6.8 fusion.123
  247.5 3.7 copy.59
  264.5 21.4 %fusion.2 = f32[12,64,16,32]{1,3,2,0:T(8,128)S(1)} fusion(f32[1024,12,32]{0,2,1:T(8,128)S(1)} %copy-done.18, f32[1024,16]{0,1:T(8,128)S(1)} %fusion.102, f32[1024,12,64]{0,2,1:T(8,128)S(1)} %bitcast.187, f32[1024,12]{0,1:T(8,128)S(1)} %copy-done.28), kind=kOutput, calls=%fused_computation.2 | convolution fusion | flops 4838916096 | bytes 6406144 | tf_op jit(solution)/shard_map/while/body/eval_jaxpr/transpose(jvp(nshf,shfd->nhd))/dot_general | solution.py:60
  286.8 49.4 %fusion = f32[12,1,16,32]{3,1,2,0:T(1,128)S(1)} fusion(f32[1024,12,32]{0,2,1:T(8,128)S(1)} %copy-done.18, f32[1024,16]{0,1:T(8,128)S(1)} %fusion.102, f32[12,1024,1,1]{1,0,2,3:T(8,128)S(1)} %get-tuple-element.155), kind=kOutput, calls=%fused_computation | convolution fusion | flops 81788928 | bytes 1712128 | tf_op jit(solution)/shard_map/while/body/eval_jaxpr/transpose(jvp(nshf,shf->nh))/dot_general | solution.py:62
  336.2 22.6 %multiply_reduce_fusion.1 = f32[12,1024,32]{1,2,0:T(8,128)S(1)} fusion(f32[12,16,32]{2,1,0:T(8,128)S(1)} %bitcast.191, f32[12,1024]{1,0:T(8,128)S(1)} %get-tuple-element.154, f32[1024,16]{0,1:T(8,128)S(1)} %fusion.102, f32[12,64,16,32]{1,3,2,0:T(8,128)S(1)} %copy-done.49, f32[1024,12,64]{0,2,1:T(8,128)S(1)} %bitcast.189, f32[1024,12]{0,1:T(8,128)S(1)} %copy-done.28), kind=kOutput, calls=%fused_computation.16 | convolution fusion | flops 4857397248 | bytes 6479872 | tf_op jit(solution)/shard_map/while/body/eval_jaxpr/transpose(jvp(nshf,shfd->nhd))/dot_general | solution.py:60
  358.8 22.8 %fusion.13 = f32[1024,12,32]{0,2,1:T(8,128)S(1)} fusion(f32[16,12,32]{2,0,1:T(8,128)S(1)} %bitcast.196, f32[1024,16]{0,1:T(8,128)S(1)} %fusion.102, f32[12,64,16,32]{1,3,2,0:T(8,128)S(1)} %fusion.2, f32[1024,3,12,64]{0,3,2,1:T(8,128)} %bitcast.181), kind=kOutput, calls=%fused_computation.15 | convolution fusion | flops 4850319360 | bytes 6381568 | tf_op jit(solution)/shard_map/while/body/eval_jaxpr/transpose(jvp(nshf,nhd->shfd))/dot_general | solution.py:57
  381.6 4.0 convolution_bitcast_fusion
  385.6 4.0 convolution_bitcast_fusion.1
  392.8 17.0 %fusion.71 = bf16[1024,1,12,64]{0,3,2,1:T(8,128)(2,1)S(1)} fusion(f32[12,64,16,32]{1,3,2,0:T(8,128)S(1)} %fusion.2, f32[1024,12,32]{0,2,1:T(8,128)S(1)} %copy-done.8, f32[1024,16]{0,1:T(8,128)S(1)} %fusion.102), kind=kOutput, calls=%fused_computation.115 | convolution fusion | flops 4838129664 | bytes 4784128 | tf_op jit(solution)/shard_map/while/body/eval_jaxpr/transpose(jvp(nshf,nhd->shfd))/dot_general | solution.py:57
  412.9 6.3 fusion.115
  419.3 10.7 %fusion.118 = f32[768,3072]{1,0:T(8,128)} fusion(bf16[1024,3072]{1,0:T(8,128)(2,1)} %copy-done.47, f32[1024,768]{0,1:T(8,128)} %copy-done.3, f32[768]{0:T(1024)S(1)} %copy-done.37, f32[768]{0:T(1024)S(1)} %convert_element_type.167, f32[1024]{0:T(1024)S(1)} %add_rsqrt_fusion, f32[1024]{0:T(1024)S(1)} %broadcast_multiply_fusion.4), kind=kOutput, calls=%fused_computation.196 | convolution fusion | flops 4835770368 | bytes 18888704 | tf_op jit(solution)/shard_map/dot_general | solution.py:101
  431.5 10.9 %fusion.124 = f32[3072,768]{1,0:T(8,128)} fusion(bf16[1024,3072]{1,0:T(8,128)(2,1)} %get-tuple-element.168, bf16[1024,768]{1,0:T(8,128)(2,1)S(1)} %copy-done.13), kind=kOutput, calls=%fused_computation.202 | convolution fusion | flops 4831838208 | bytes 17301504 | tf_op jit(solution)/shard_map/dot_general | solution.py:101
  444.8 9.8 %fusion.122 = (f32[768]{0:T(1024)S(1)}, f32[1024,768]{1,0:T(8,128)}) fusion(bf16[1024,2304]{0,1:T(8,128)(2,1)} %bitcast.186, bf16[768,2304]{1,0:T(8,128)(2,1)} %all-gather.5.cloned.1.call-done), kind=kOutput, calls=%fused_computation.200 | convolution fusion | flops 3624664320 | bytes 11406336 | tf_op jit(solution)/shard_map/dot_general | solution.py:107
  454.6 3.5 copy.60
  461.0 59.4 %all-reduce.20 = (bf16[2304]{0:T(1024)(128)(2,1)S(1)}, bf16[768]{0:T(1024)(128)(2,1)S(1)}, bf16[768]{0:T(1024)(128)(2,1)S(1)}, bf16[768]{0:T(1024)(128)(2,1)S(1)...) all-reduce(f32[2304]{0:T(1024)S(1)} %reshape.194, ...), channel_id=5, replica_groups=mesh['fsdp'=16,'dp'=2] {'fsdp'}, use_global_device_ids=true, to_apply=%region_23.25.clone | all-reduce | flops 9984 | bytes 59904
  521.0 4.9 all-reduce.22
  530.6 10.9 %add_convert_fusion = bf16[1024,768]{0,1:T(8,128)(2,1)} fusion(f32[1024,768]{0,1:T(8,128)} %copy-done.3, bf16[1024,3072]{1,0:T(8,128)(2,1)} %get-tuple-element.168, bf16[3072,768]{1,0:T(8,128)(2,1)} %all-gather.11.cloned.1.call-done, f32[768]{0:T(1024)S(1)} %convert_element_type.172), kind=kOutput, calls=%fused_computation.109 | convolution fusion | flops 4834197504 | bytes 15731712 | tf_op jit(solution)/shard_map/dot_general | solution.py:200
  544.9 77.4 %reduce-scatter.9.cloned.1.call-done = f32[48,3072]{1,0:T(8,128)} async-done(((f32[768,3072]{1,0:T(8,128)}), f32[48,3072]{1,0:T(8,128)}) %reduce-scatter.9.cloned.1.call-update) | async-done | bytes 589840 | tf_op jit(solution)/shard_map/reduce_scatter | solution.py:138
  624.2 114.0 %reduce-scatter.11.cloned.1.call-done = f32[192,768]{1,0:T(8,128)} async-done(((f32[3072,768]{1,0:T(8,128)}), f32[192,768]{1,0:T(8,128)}) %reduce-scatter.11.cloned.1.call-update) | async-done | bytes 589840 | tf_op jit(solution)/shard_map/reduce_scatter | solution.py:140
  740.0 3.9 fusion.54
  747.0 31.6 %all-reduce.26.cloned.1.call-done = (bf16[48,2304]{1,0:T(8,128)(2,1)}, bf16[48,768]{1,0:T(8,128)(2,1)}, bf16[48,3072]{1,0:T(8,128)(2,1)}, bf16[192,768]{1,0:T(8,128)(2,1)}) async-done(((bf16[48,2304]{1,0:T(8,128)(2,1)}, bf16[48,768]{1,0:T(8,128)(2,1)}, bf16[48,3072]{1,0:T(8,128)(2,1)}, bf16[192,768]{1,0:T(8,128)(2,1)}), (bf16[48,2304]{1,0:T(8,128)(2,1)}, bf16[48,768]{1,0:T(8,128)(2,1)}, ...) | async-done | bytes 884752 | tf_op jit(solution)/shard_map/psum | solution.py:146
  (222 shorter events, 79.0 us)
Async XLA Ops:
  7.2 111.2 %copy-start = (f32[12,32,64]{2,1,0:T(8,128)S(1)}, f32[12,32,64]{2,1,0:T(8,128)}, u32[]{:S(2)}) copy-start(f32[12,32,64]{2,1,0:T(8,128)} %param.19) | copy-start | bytes 294916
  7.2 87.5 %all-gather.5.cloned.1.call-start = ((), (), s32[]{:S(2)}) async-start(), calls=%async_computation.4 | async-start | bytes 3760128 | tf_op jit(solution)/shard_map/all_gather | solution.py:116
  7.9 176.4 %all-gather.7.cloned.1.call-start = ((), (), s32[]{:S(2)}) async-start(), calls=%async_computation.5 | async-start | bytes 1253376 | tf_op jit(solution)/shard_map/all_gather | solution.py:118
  8.7 181.2 %all-gather.9.cloned.1.call-start = ((), (), s32[]{:S(2)}) async-start(), calls=%async_computation.6 | async-start | bytes 5013504 | tf_op jit(solution)/shard_map/all_gather | solution.py:116
  9.4 219.4 %all-gather.11.cloned.1.call-start = ((), (), s32[]{:S(2)}) async-start(), calls=%async_computation.7 | async-start | bytes 5013504 | tf_op jit(solution)/shard_map/all_gather | solution.py:118
  10.0 531.5 %reduce-scatter.7.cloned.1.call-start = ((), (), s32[]{:S(2)}) async-start(), calls=%async_computation.9 | async-start | bytes 2506752 | tf_op jit(solution)/shard_map/reduce_scatter | solution.py:140
  85.5 9.2 %copy-start.29 = (f32[768]{0:T(1024)}, f32[768]{0:T(1024)S(1)}, u32[]{:S(2)}) copy-start(f32[768]{0:T(1024)S(1)} %convert_element_type.159) | copy-start | bytes 9220
  86.7 6.3 copy-start.12
  88.5 95.8 %copy-start.1 = (bf16[1024,768]{0,1:T(8,128)(2,1)}, bf16[1024,768]{0,1:T(8,128)(2,1)S(1)}, u32[]{:S(2)}) copy-start(bf16[1024,768]{0,1:T(8,128)(2,1)S(1)} %copy.55) | copy-start | bytes 4718596
  88.9 14.4 %copy-start.25 = (f32[1024]{0:T(1024)}, f32[1024]{0:T(1024)S(1)}, u32[]{:S(2)}) copy-start(f32[1024]{0:T(1024)S(1)} %broadcast_multiply_fusion.5) | copy-start | bytes 12292
  89.3 13.9 %copy-start.31 = (f32[1024]{0:T(1024)}, f32[1024]{0:T(1024)S(1)}, u32[]{:S(2)}) copy-start(f32[1024]{0:T(1024)S(1)} %add_rsqrt_fusion.1) | copy-start | bytes 12292
  90.6 26.3 %copy-start.19 = (f32[1024,32]{0,1:T(8,128)}, f32[1024,32]{0,1:T(8,128)S(1)}, u32[]{:S(2)}) copy-start(f32[1024,32]{0,1:T(8,128)S(1)} %get-tuple-element.158) | copy-start | bytes 393220
  113.0 9.1 %slice-start = ((s8[9437184]{0:T(1024)(128)(4,1)}), s8[4194304]{0:T(1024)(128)(4,1)S(1)}, s32[]{:S(2)}) async-start(s8[9437184]{0:T(1024)(128)(4,1)} %bitcast.182), calls=%async_computation.13 | async-start | bytes 8388608
  113.0 9.1 %slice-start.1 = ((s8[9437184]{0:T(1024)(128)(4,1)}), s8[4194304]{0:T(1024)(128)(4,1)S(1)}, s32[]{:S(2)}) async-start(s8[9437184]{0:T(1024)(128)(4,1)} %bitcast.182), calls=%async_computation.14 | async-start | bytes 8388608
  116.8 5.2 slice-start.2
  122.0 21.6 %copy-start.7 = (f32[1024,12,32]{0,2,1:T(8,128)}, f32[1024,12,32]{0,2,1:T(8,128)S(1)}, u32[]{:S(2)}) copy-start(f32[1024,12,32]{0,2,1:T(8,128)S(1)} %get-tuple-element.162) | copy-start | bytes 4718596
  143.7 21.7 %copy-start.48 = (f32[12,64,16,32]{1,3,2,0:T(8,128)}, f32[12,64,16,32]{1,3,2,0:T(8,128)S(1)}, u32[]{:S(2)}) copy-start(f32[12,64,16,32]{1,3,2,0:T(8,128)S(1)} %fusion.10) | copy-start | bytes 4718596
  149.3 16.1 %copy-start.17 = (f32[1024,12,32]{0,2,1:T(8,128)}, f32[1024,12,32]{0,2,1:T(8,128)S(1)}, u32[]{:S(2)}) copy-start(f32[1024,12,32]{0,2,1:T(8,128)S(1)} %get-tuple-element.160) | copy-start | bytes 4718596
  149.3 16.0 %copy-start.33 = (f32[1024]{0:T(1024)S(1)}, f32[1024]{0:T(1024)}, u32[]{:S(2)}) copy-start(f32[1024]{0:T(1024)} %broadcast_subtract_fusion) | copy-start | bytes 12292
  166.0 18.3 %copy-start.38 = (f32[768]{0:T(1024)S(1)}, f32[768]{0:T(1024)}, u32[]{:S(2)}) copy-start(f32[768]{0:T(1024)} %convert_element_type.166) | copy-start | bytes 9220
  228.8 11.9 %copy-start.44 = (bf16[768,3072]{1,0:T(8,128)(2,1)S(1)}, bf16[768,3072]{1,0:T(8,128)(2,1)}, u32[]{:S(2)}) copy-start(bf16[768,3072]{1,0:T(8,128)(2,1)} %all-gather.9.cloned.1.call-done) | copy-start | bytes 14155780
  240.7 6.8 copy-start.47
  261.0 282.1 %reduce-scatter.5.cloned.1.call-start = ((), (), s32[]{:S(2)}) async-start(), calls=%async_computation.8 | async-start | bytes 7520256 | tf_op jit(solution)/shard_map/reduce_scatter | solution.py:138
  264.4 21.4 %copy-start.11 = (f32[12,64,1024,1]{2,1,3,0:T(8,128)S(1)}, f32[12,64,1024,1]{2,1,3,0:T(8,128)}, u32[]{:S(2)}) copy-start(f32[12,64,1024,1]{2,1,3,0:T(8,128)} %get-tuple-element.165) | copy-start | bytes 9437188
  286.8 49.4 %copy-start.24 = (f32[16,12,32]{2,0,1:T(8,128)S(1)}, f32[16,12,32]{2,0,1:T(8,128)}, u32[]{:S(2)}) copy-start(f32[16,12,32]{2,0,1:T(8,128)} %copy-done.23) | copy-start | bytes 73732
  286.8 49.4 %copy-start.49 = (f32[12,64,16,32]{1,3,2,0:T(8,128)S(1)}, f32[12,64,16,32]{1,3,2,0:T(8,128)}, u32[]{:S(2)}) copy-start(f32[12,64,16,32]{1,3,2,0:T(8,128)} %copy-done.48) | copy-start | bytes 4718596
  358.8 22.8 %copy-start.15 = (f32[12,1024,32]{1,2,0:T(8,128)S(1)}, f32[12,1024,32]{1,2,0:T(8,128)}, u32[]{:S(2)}) copy-start(f32[12,1024,32]{1,2,0:T(8,128)} %get-tuple-element.163) | copy-start | bytes 4718596
  385.6 4.0 copy-start.20
  385.6 4.0 copy-start.22
  419.2 203.1 %reduce-scatter.9.cloned.1.call-start = ((), (), s32[]{:S(2)}) async-start(), calls=%async_computation.10 | async-start | bytes 10027008 | tf_op jit(solution)/shard_map/reduce_scatter | solution.py:138
  430.0 308.2 %reduce-scatter.11.cloned.1.call-start = ((), (), s32[]{:S(2)}) async-start(), calls=%async_computation.11 | async-start | bytes 10027008 | tf_op jit(solution)/shard_map/reduce_scatter | solution.py:140
  442.4 336.2 %all-reduce.26.cloned.1.call-start = ((), (), s32[]{:S(2)}) async-start(), calls=%async_computation.12 | async-start | bytes 1769472 | tf_op jit(solution)/shard_map/psum | solution.py:146
  (30 other events, 80.8 us)
Sparse Core Ops, SparseCore 0:
  10.3 50.8 all-gather.4
  63.5 36.6 all-gather.6
  102.5 52.2 all-gather.8
  156.9 51.7 all-gather.10
  261.1 60.1 reduce-scatter.6
  419.3 87.8 reduce-scatter.4
  511.3 110.9 reduce-scatter.8
  627.0 111.0 reduce-scatter.10
  741.8 36.7 all-reduce.25
where the time goes:
time: 801 us; the launch traced here: 793 us
  matrix products  329 us (41%)
  waiting for transfers between devices  226 us (28%)
  blocking collectives  128 us (16%)
  local copies, waits for them, and re-layouts  46.5 us (6%)
  other arithmetic  44.3 us (6%)
  between operations  19.1 us (2%)
    unnamed x2, blocking collectives  123 us
    reduce_scatter x2, waiting for transfers between devices, reduce_grads(): lax.psum_scatter(grads[4], 'fsdp', scatter_dimension=0, tiled=True)  114 us
    reduce_scatter x2, waiting for transfers between devices, reduce_grads(): lax.psum_scatter(grads[2], 'fsdp', scatter_dimension=0, tiled=True)  77.4 us
    dot_general x2, matrix products, segment_core(): jnp.einsum('nshf,shf->nh', masked_queries, totals, precision=highest)  65.4 us
    dot_general x3, matrix products, segment_core(): jnp.einsum('nshf,shfd->nhd', masked_queries, kv_state, precision=highest)  62.4 us
    dot_general x3, matrix products, segment_core(): jnp.einsum('nshf,nhd->shfd', masked_keys, value_rows, precision=highest)  61.4 us
    dot_general x1, matrix products, body(): jnp.dot(hidden_two, weight_in, preferred_element_type=jnp.float32)  38.9 us
    dot_general x4, matrix products, contract_cols(): lax.dot_general(left, right, (((1,), (1,)), ((), ())), preferred_element_...  31.8 us
  transfers between devices with their start and end apart: 9, of which 3 were waited for; matrix products, arithmetic and copies ran while one was open for 47% of the time, Pallas kernels for 0%

commit v1 on v0

--- a/solution.py
+++ b/solution.py
@@ -8,6 +8,11 @@
 SEGS = 16
 highest = lax.Precision.HIGHEST
 epsilon = 1e-05
+
+
+def add_all(array, mesh_axis):
+    terms = lax.all_gather(array, mesh_axis)
+    return jnp.sum(terms, axis=0)
 
 
 def norm_forward(rows, gain, shift):
@@ -143,7 +148,7 @@
     return (
         lax.psum(pieces[0].astype(jnp.bfloat16), "dp").astype(jnp.float32),
         lax.psum(pieces[1].astype(jnp.bfloat16), "dp").astype(jnp.float32),
-        lax.psum(pieces[2].astype(jnp.bfloat16), "dp").astype(jnp.float32),
+        add_all(pieces[2].astype(jnp.bfloat16), "dp").astype(jnp.float32),
         lax.psum(pieces[3].astype(jnp.bfloat16), "dp").astype(jnp.float32),
         lax.psum(pieces[4].astype(jnp.bfloat16), "dp").astype(jnp.float32),
         lax.psum(pieces[5].astype(jnp.bfloat16), "dp").astype(jnp.float32),

time: 801 us -> 695 us (0.87)
  waiting for transfers between devices: 226 us -> 107 us
  blocking collectives: 128 us -> 145 us
    reduce_scatter x2, waiting for transfers between devices: 114 us -> 0.02 us  [reduce_grads(): lax.psum_scatter(grads[4], 'fsdp', scatter_dimension=0, tiled=True)]
    all_gather x0 -> x2, blocking collectives: none -> 16.9 us  [add_all(): terms = lax.all_gather(array, mesh_axis)]
    psum x1, waiting for transfers between devices: 31.6 us -> 16.2 us  [reduce_grads(): lax.psum(pieces[4].astype(jnp.bfloat16), 'dp').astype(jnp.float32)]
    reduce_scatter x2, waiting for transfers between devices: 77.4 us -> 88.5 us  [reduce_grads(): lax.psum_scatter(grads[2], 'fsdp', scatter_dimension=0, tiled=True)]
    unnamed x135 -> x143, local copies, waits for them, and re-layouts: 24.5 us -> 25.4 us
  transfers between devices with their start and end apart: 9 -> 9, of which waited for: 3 -> 2; matrix products, arithmetic and copies ran while one was open for 47% -> 54% of each run, Pallas kernels for 0% -> 0%
where the time goes in v1:
time: 695 us; the launch traced here: 686 us
  matrix products  325 us (47%)
  blocking collectives  145 us (21%)
  waiting for transfers between devices  107 us (15%)
  local copies, waits for them, and re-layouts  47.7 us (7%)
  other arithmetic  40.4 us (6%)
  between operations  19.1 us (3%)
    unnamed x2, blocking collectives  124 us
    reduce_scatter x2, waiting for transfers between devices, reduce_grads(): lax.psum_scatter(grads[2], 'fsdp', scatter_dimension=0, tiled=True)  88.5 us
    dot_general x2, matrix products, segment_core(): jnp.einsum('nshf,shf->nh', masked_queries, totals, precision=highest)  65.2 us
    dot_general x3, matrix products, segment_core(): jnp.einsum('nshf,shfd->nhd', masked_queries, kv_state, precision=highest)  62.2 us
    dot_general x3, matrix products, segment_core(): jnp.einsum('nshf,nhd->shfd', masked_keys, value_rows, precision=highest)  60.8 us
    dot_general x1, matrix products, body(): jnp.dot(hidden_two, weight_in, preferred_element_type=jnp.float32)  38.9 us
    dot_general x4, matrix products, contract_cols(): lax.dot_general(left, right, (((1,), (1,)), ((), ())), preferred_element_...  32 us
    dot_general x4, matrix products, contract_rows(): lax.dot_general(left, right, (((0,), (0,)), ((), ())), preferred_element_...  30.3 us
  transfers between devices with their start and end apart: 9, of which 2 were waited for; matrix products, arithmetic and copies ran while one was open for 54% of the time, Pallas kernels for 0%

profile of v1, /device:TPU:0, one launch (start us, length us, event | category | flops | bytes accessed | tf_op | source)
XLA Modules:
  0.0 685.7 jit_solution(5106083203645284273)
XLA Ops:
  22.0 63.5 %all-reduce.21 = (bf16[2304]{0:T(1024)(128)(2,1)S(1)}, bf16[768]{0:T(1024)(128)(2,1)S(1)}, bf16[768]{0:T(1024)(128)(2,1)S(1)}, bf16[768]{0:T(1024)(128)(2,1)}, b...) all-reduce(bf16[2304]{0:T(1024)(128)(2,1)S(1)} %dynamic-update-slic, ...), channel_id=1, replica_groups=mesh['fsdp'=16,'dp'=2] {'fsdp'}, use_global_device_ids=true, to_apply=%add.6 | all-reduce | flops 9984 | bytes 39936
  94.6 8.6 %convolution_add_fusion = f32[1024,2304]{1,0:T(8,128)} fusion(bf16[768,2304]{1,0:T(8,128)(2,1)} %all-gather.7.cloned.1.call-done, f32[2304]{0:T(1024)} %convert_element_type.166, bf16[1024,768]{0,1:T(8,128)(2,1)S(1)} %copy.55, f32[768]{0:T(1024)} %convert_element_type.164, f32[768]{0:T(1024)S(1)} %convert_element_type.163, f32[1024]{0:T(1024)S(1)} %add_rsqrt_fusion.1, ...), kind=kOutput, calls=%fused_computation.58 | convolution fusion | flops 3630956544 | bytes 14572544 | tf_op jit(solution)/shard_map/dot_general | solution.py:187
  103.2 9.6 %copy.56 = f32[1024,2304]{0,1:T(8,128)} copy(f32[1024,2304]{1,0:T(8,128)} %convolution_add_fusion) | data formatting | bytes 18874368 | tf_op jit(solution)/shard_map/add | solution.py:187
  112.8 3.8 slice_bitcast_fusion.1
  118.2 3.7 compare_select_fusion.5
  121.9 21.4 %fusion.10 = f32[12,64,16,32]{1,3,2,0:T(8,128)S(1)} fusion(f32[1024,12,32]{0,2,1:T(8,128)S(1)} %get-tuple-element.160, f32[1024,16]{0,1:T(8,128)S(1)} %fusion.102, f32[1024,3,12,64]{0,3,2,1:T(8,128)S(1)} %bitcast.186), kind=kOutput, calls=%fused_computation.11 | convolution fusion | flops 4838129664 | bytes 6356992 | tf_op jit(solution)/shard_map/while/body/eval_jaxpr/nshf,nhd->shfd/dot_general | solution.py:62
  145.2 3.7 compare_select_fusion.4
  148.9 16.0 %fusion.4 = f32[12,1,1024,1]{2,1,3,0:T(1,128)S(1)} fusion(f32[16,12,32,1]{2,3,0,1:T(1,128)S(1)} %bitcast.194, f32[1024,12,32]{0,2,1:T(8,128)S(1)} %get-tuple-element.158, f32[1024,16]{0,1:T(8,128)S(1)} %fusion.102), kind=kOutput, calls=%fused_computation.4 | convolution fusion | flops 81788928 | bytes 1712128 | tf_op jit(solution)/shard_map/while/body/eval_jaxpr/nshf,shf->nh/dot_general | solution.py:67
  165.0 18.6 %fusion.65 = (bf16[1024,12,64]{0,2,1:T(8,128)(2,1)}, f32[12,64,1024,1]{2,1,3,0:T(8,128)}) fusion(f32[1024,12]{0,1:T(8,128)S(1)} %fusion.101, f32[1024,12,32]{0,2,1:T(8,128)S(1)} %get-tuple-element.158, f32[1024,16]{0,1:T(8,128)S(1)} %fusion.102, f32[12,64,16,32]{1,3,2,0:T(8,128)S(1)} %fusion.10), kind=kOutput, calls=%fused_computation.98 | convolution fusion | flops 4839702528 | bytes 7979008 | tf_op jit(solution)/shard_map/while/body/eval_jaxpr/nshf,shfd->nhd/dot_general | solution.py:65
  189.2 38.9 %fusion.16 = (bf16[1024,3072]{1,0:T(8,128)(2,1)}, f32[1024,3072]{1,0:T(8,128)}) fusion(f32[3072]{0:T(1024)S(1)} %copy-done.36, bf16[768,3072]{1,0:T(8,128)(2,1)} %all-gather.11.cloned.1.call-done, f32[1024,768]{0,1:T(8,128)} %copy-done.3, f32[768]{0:T(1024)S(1)} %copy-done.41, f32[768]{0:T(1024)S(1)} %convert_element_type.171, f32[1024]{0:T(1024)S(1)} %add_rsqrt_fusion, ...), kind=kOutput, calls=%fused_computation.21 | convolution fusion | flops 5043388416 | bytes 26765312 | tf_op jit(solution)/shard_map/dot_general | solution.py:201
  228.1 12.5 %convert_reduce_fusion = (f32[3072]{0:T(1024)}, bf16[1024,3072]{1,0:T(8,128)(2,1)S(1)}) fusion(f32[1024,3072]{1,0:T(8,128)} %get-tuple-element.167, f32[3072]{0:T(1024)S(1)} %copy-done.36, bf16[1024,768]{1,0:T(8,128)(2,1)S(1)} %copy-done.15, bf16[3072,768]{1,0:T(8,128)(2,1)} %all-gather.13.cloned.1.call-done), kind=kOutput, calls=%fused_computation.28 | convolution fusion | flops 4872729600 | bytes 25190400 | tf_op jit(solution)/shard_map/dot_general | solution.py:112
  240.6 7.3 %fusion.123 = (f32[768]{0:T(1024)}, f32[1024,768]{1,0:T(8,128)}) fusion(bf16[1024,3072]{1,0:T(8,128)(2,1)S(1)} %get-tuple-element.173, bf16[768,3072]{1,0:T(8,128)(2,1)S(1)} %copy-done.49), kind=kOutput, calls=%fused_computation.201 | convolution fusion | flops 4832623616 | bytes 14158848 | tf_op jit(solution)/shard_map/dot_general | solution.py:112
  247.9 3.7 copy.59
  261.3 10.3 %fusion.124 = f32[3072,768]{1,0:T(8,128)} fusion(bf16[1024,3072]{1,0:T(8,128)(2,1)} %get-tuple-element.166, bf16[1024,768]{1,0:T(8,128)(2,1)S(1)} %copy-done.16), kind=kOutput, calls=%fused_computation.202 | convolution fusion | flops 4831838208 | bytes 17301504 | tf_op jit(solution)/shard_map/dot_general | solution.py:106
  277.9 49.1 %fusion = f32[12,1,16,32]{3,1,2,0:T(1,128)S(1)} fusion(f32[1024,12,32]{0,2,1:T(8,128)S(1)} %copy-done.20, f32[1024,16]{0,1:T(8,128)S(1)} %fusion.102, f32[12,1024,1,1]{1,0,2,3:T(8,128)S(1)} %get-tuple-element.153), kind=kOutput, calls=%fused_computation | convolution fusion | flops 81788928 | bytes 1712128 | tf_op jit(solution)/shard_map/while/body/eval_jaxpr/transpose(jvp(nshf,shf->nh))/dot_general | solution.py:67
  327.0 20.8 %fusion.2 = f32[12,64,16,32]{1,3,2,0:T(8,128)S(1)} fusion(f32[1024,12,32]{0,2,1:T(8,128)S(1)} %copy-done.20, f32[1024,16]{0,1:T(8,128)S(1)} %fusion.102, f32[1024,12,64]{0,2,1:T(8,128)S(1)} %bitcast.190, f32[1024,12]{0,1:T(8,128)S(1)} %copy-done.30), kind=kOutput, calls=%fused_computation.2 | convolution fusion | flops 4838916096 | bytes 6406144 | tf_op jit(solution)/shard_map/while/body/eval_jaxpr/transpose(jvp(nshf,shfd->nhd))/dot_general | solution.py:65
  347.8 22.9 %fusion.13 = f32[1024,12,32]{0,2,1:T(8,128)S(1)} fusion(f32[16,12,32]{2,0,1:T(8,128)S(1)} %bitcast.200, f32[1024,16]{0,1:T(8,128)S(1)} %fusion.102, f32[12,64,16,32]{1,3,2,0:T(8,128)S(1)} %fusion.2, f32[1024,3,12,64]{0,3,2,1:T(8,128)} %bitcast.183), kind=kOutput, calls=%fused_computation.15 | convolution fusion | flops 4850319360 | bytes 6381568 | tf_op jit(solution)/shard_map/while/body/eval_jaxpr/transpose(jvp(nshf,nhd->shfd))/dot_general | solution.py:62
  370.7 3.9 convolution_bitcast_fusion
  374.7 22.9 %multiply_reduce_fusion.1 = f32[12,1024,32]{1,2,0:T(8,128)S(1)} fusion(f32[12,16,32]{2,1,0:T(8,128)S(1)} %bitcast.195, f32[12,1024]{1,0:T(8,128)S(1)} %get-tuple-element.152, f32[1024,16]{0,1:T(8,128)S(1)} %fusion.102, f32[12,64,16,32]{1,3,2,0:T(8,128)S(1)} %copy-done.53, f32[1024,12,64]{0,2,1:T(8,128)S(1)} %bitcast.191, f32[1024,12]{0,1:T(8,128)S(1)} %copy-done.30), kind=kOutput, calls=%fused_computation.16 | convolution fusion | flops 4857397248 | bytes 6479872 | tf_op jit(solution)/shard_map/while/body/eval_jaxpr/transpose(jvp(nshf,shfd->nhd))/dot_general | solution.py:65
  397.6 3.9 convolution_bitcast_fusion.1
  404.1 16.5 %fusion.71 = bf16[1024,1,12,64]{0,3,2,1:T(8,128)(2,1)S(1)} fusion(f32[12,64,16,32]{1,3,2,0:T(8,128)S(1)} %fusion.2, f32[1024,12,32]{0,2,1:T(8,128)S(1)} %copy-done.11, f32[1024,16]{0,1:T(8,128)S(1)} %fusion.102), kind=kOutput, calls=%fused_computation.115 | convolution fusion | flops 4838129664 | bytes 4784128 | tf_op jit(solution)/shard_map/while/body/eval_jaxpr/transpose(jvp(nshf,nhd->shfd))/dot_general | solution.py:62
  423.8 6.4 fusion.115
  430.8 10.8 %fusion.118 = f32[768,3072]{1,0:T(8,128)} fusion(bf16[1024,3072]{1,0:T(8,128)(2,1)} %copy-done.51, f32[1024,768]{0,1:T(8,128)} %copy-done.3, f32[768]{0:T(1024)S(1)} %copy-done.42, f32[768]{0:T(1024)S(1)} %convert_element_type.171, f32[1024]{0:T(1024)S(1)} %add_rsqrt_fusion, f32[1024]{0:T(1024)S(1)} %broadcast_multiply_fusion.4), kind=kOutput, calls=%fused_computation.196 | convolution fusion | flops 4835770368 | bytes 18888704 | tf_op jit(solution)/shard_map/dot_general | solution.py:106
  444.1 9.4 %fusion.122 = (f32[768]{0:T(1024)S(1)}, f32[1024,768]{1,0:T(8,128)}) fusion(bf16[1024,2304]{0,1:T(8,128)(2,1)} %bitcast.188, bf16[768,2304]{1,0:T(8,128)(2,1)} %all-gather.7.cloned.1.call-done), kind=kOutput, calls=%fused_computation.200 | convolution fusion | flops 3624664320 | bytes 11406336 | tf_op jit(solution)/shard_map/dot_general | solution.py:112
  453.4 3.8 copy.60
  463.8 8.6 %add_convert_fusion = bf16[1024,768]{0,1:T(8,128)(2,1)S(1)} fusion(f32[1024,768]{0,1:T(8,128)S(1)} %copy-done.5, bf16[1024,3072]{1,0:T(8,128)(2,1)} %get-tuple-element.166, bf16[3072,768]{1,0:T(8,128)(2,1)} %all-gather.13.cloned.1.call-done, f32[768]{0:T(1024)S(1)} %convert_element_type.176), kind=kOutput, calls=%fused_computation.109 | convolution fusion | flops 4834197504 | bytes 15731712 | tf_op jit(solution)/shard_map/dot_general | solution.py:205
  476.1 60.0 %all-reduce.20 = (bf16[2304]{0:T(1024)(128)(2,1)S(1)}, bf16[768]{0:T(1024)(128)(2,1)S(1)}, bf16[768]{0:T(1024)(128)(2,1)S(1)}, bf16[768]{0:T(1024)(128)(2,1)S(1)...) all-reduce(f32[2304]{0:T(1024)S(1)} %reshape.194, ...), channel_id=7, replica_groups=mesh['fsdp'=16,'dp'=2] {'fsdp'}, use_global_device_ids=true, to_apply=%region_23.25.clone | all-reduce | flops 9984 | bytes 59904
  536.7 4.9 all-reduce.22
  550.6 6.6 all-gather
  558.2 88.5 %reduce-scatter.9.cloned.1.call-done = f32[48,3072]{1,0:T(8,128)} async-done(((f32[768,3072]{1,0:T(8,128)}), f32[48,3072]{1,0:T(8,128)}) %reduce-scatter.9.cloned.1.call-update) | async-done | bytes 589840 | tf_op jit(solution)/shard_map/reduce_scatter | solution.py:143
  647.7 10.3 %all-gather.1 = bf16[96,3072]{1,0:T(8,128)(2,1)S(1)} all-gather(bf16[48,3072]{1,0:T(8,128)(2,1)S(1)} %convert_element_type.202), channel_id=3, replica_groups=mesh['fsdp'=16,'dp'=2] {'dp'}, dimensions={0}, use_global_device_ids=true | all-gather | bytes 884736 | tf_op jit(solution)/shard_map/all_gather | solution.py:14
  659.1 16.2 %all-reduce.26.cloned.1.call-done = (bf16[48,768]{1,0:T(8,128)(2,1)}, bf16[192,768]{1,0:T(8,128)(2,1)}) async-done(((bf16[48,768]{1,0:T(8,128)(2,1)}, bf16[192,768]{1,0:T(8,128)(2,1)}), (bf16[48,768]{1,0:T(8,128)(2,1)}, bf16[192,768]{1,0:T(8,128)(2,1)})) %all-reduce.26.cloned.1.call-update) | async-done | bytes 368656 | tf_op jit(solution)/shard_map/psum | solution.py:153
  (234 shorter events, 79.6 us)
Async XLA Ops:
  7.2 111.0 %copy-start = (f32[12,32,64]{2,1,0:T(8,128)S(1)}, f32[12,32,64]{2,1,0:T(8,128)}, u32[]{:S(2)}) copy-start(f32[12,32,64]{2,1,0:T(8,128)} %param.19) | copy-start | bytes 294916
  7.2 87.4 %all-gather.7.cloned.1.call-start = ((), (), s32[]{:S(2)}) async-start(), calls=%async_computation.4 | async-start | bytes 3760128 | tf_op jit(solution)/shard_map/all_gather | solution.py:121
  7.9 175.7 %all-gather.9.cloned.1.call-start = ((), (), s32[]{:S(2)}) async-start(), calls=%async_computation.5 | async-start | bytes 1253376 | tf_op jit(solution)/shard_map/all_gather | solution.py:123
  8.7 180.5 %all-gather.11.cloned.1.call-start = ((), (), s32[]{:S(2)}) async-start(), calls=%async_computation.6 | async-start | bytes 5013504 | tf_op jit(solution)/shard_map/all_gather | solution.py:121
  9.4 218.7 %all-gather.13.cloned.1.call-start = ((), (), s32[]{:S(2)}) async-start(), calls=%async_computation.7 | async-start | bytes 5013504 | tf_op jit(solution)/shard_map/all_gather | solution.py:123
  10.0 462.5 %reduce-scatter.7.cloned.1.call-start = ((), (), s32[]{:S(2)}) async-start(), calls=%async_computation.9 | async-start | bytes 2506752 | tf_op jit(solution)/shard_map/reduce_scatter | solution.py:145
  85.5 9.1 %copy-start.31 = (f32[768]{0:T(1024)}, f32[768]{0:T(1024)S(1)}, u32[]{:S(2)}) copy-start(f32[768]{0:T(1024)S(1)} %convert_element_type.163) | copy-start | bytes 9220
  86.7 6.3 copy-start.15
  88.5 95.1 %copy-start.1 = (bf16[1024,768]{0,1:T(8,128)(2,1)}, bf16[1024,768]{0,1:T(8,128)(2,1)S(1)}, u32[]{:S(2)}) copy-start(bf16[1024,768]{0,1:T(8,128)(2,1)S(1)} %copy.55) | copy-start | bytes 4718596
  88.9 14.3 %copy-start.27 = (f32[1024]{0:T(1024)}, f32[1024]{0:T(1024)S(1)}, u32[]{:S(2)}) copy-start(f32[1024]{0:T(1024)S(1)} %broadcast_multiply_fusion.5) | copy-start | bytes 12292
  89.3 13.8 %copy-start.33 = (f32[1024]{0:T(1024)}, f32[1024]{0:T(1024)S(1)}, u32[]{:S(2)}) copy-start(f32[1024]{0:T(1024)S(1)} %add_rsqrt_fusion.1) | copy-start | bytes 12292
  90.6 26.1 %copy-start.21 = (f32[1024,32]{0,1:T(8,128)}, f32[1024,32]{0,1:T(8,128)S(1)}, u32[]{:S(2)}) copy-start(f32[1024,32]{0,1:T(8,128)S(1)} %get-tuple-element.156) | copy-start | bytes 393220
  112.8 9.1 %slice-start = ((s8[9437184]{0:T(1024)(128)(4,1)}), s8[4194304]{0:T(1024)(128)(4,1)S(1)}, s32[]{:S(2)}) async-start(s8[9437184]{0:T(1024)(128)(4,1)} %bitcast.184), calls=%async_computation.13 | async-start | bytes 8388608
  112.8 9.1 %slice-start.1 = ((s8[9437184]{0:T(1024)(128)(4,1)}), s8[4194304]{0:T(1024)(128)(4,1)S(1)}, s32[]{:S(2)}) async-start(s8[9437184]{0:T(1024)(128)(4,1)} %bitcast.184), calls=%async_computation.14 | async-start | bytes 8388608
  116.7 5.2 slice-start.2
  121.9 21.4 %copy-start.10 = (f32[1024,12,32]{0,2,1:T(8,128)}, f32[1024,12,32]{0,2,1:T(8,128)S(1)}, u32[]{:S(2)}) copy-start(f32[1024,12,32]{0,2,1:T(8,128)S(1)} %get-tuple-element.160) | copy-start | bytes 4718596
  143.3 21.7 %copy-start.52 = (f32[12,64,16,32]{1,3,2,0:T(8,128)}, f32[12,64,16,32]{1,3,2,0:T(8,128)S(1)}, u32[]{:S(2)}) copy-start(f32[12,64,16,32]{1,3,2,0:T(8,128)S(1)} %fusion.10) | copy-start | bytes 4718596
  148.9 16.1 %copy-start.19 = (f32[1024,12,32]{0,2,1:T(8,128)}, f32[1024,12,32]{0,2,1:T(8,128)S(1)}, u32[]{:S(2)}) copy-start(f32[1024,12,32]{0,2,1:T(8,128)S(1)} %get-tuple-element.158) | copy-start | bytes 4718596
  148.9 16.0 %copy-start.35 = (f32[1024]{0:T(1024)S(1)}, f32[1024]{0:T(1024)}, u32[]{:S(2)}) copy-start(f32[1024]{0:T(1024)} %broadcast_subtract_fusion) | copy-start | bytes 12292
  165.0 18.6 %copy-start.29 = (f32[1024,12]{0,1:T(8,128)}, f32[1024,12]{0,1:T(8,128)S(1)}, u32[]{:S(2)}) copy-start(f32[1024,12]{0,1:T(8,128)S(1)} %fusion.101) | copy-start | bytes 147460
  165.0 18.6 %copy-start.43 = (f32[768]{0:T(1024)S(1)}, f32[768]{0:T(1024)}, u32[]{:S(2)}) copy-start(f32[768]{0:T(1024)} %convert_element_type.170) | copy-start | bytes 9220
  228.1 12.5 %copy-start.49 = (bf16[768,3072]{1,0:T(8,128)(2,1)S(1)}, bf16[768,3072]{1,0:T(8,128)(2,1)}, u32[]{:S(2)}) copy-start(bf16[768,3072]{1,0:T(8,128)(2,1)} %all-gather.11.cloned.1.call-done) | copy-start | bytes 14155780
  240.6 7.3 %copy-start.51 = (bf16[1024,3072]{1,0:T(8,128)(2,1)}, bf16[1024,3072]{1,0:T(8,128)(2,1)S(1)}, u32[]{:S(2)}) copy-start(bf16[1024,3072]{1,0:T(8,128)(2,1)S(1)} %get-tuple-element.173) | copy-start | bytes 18874372
  261.2 212.9 %reduce-scatter.11.cloned.1.call-start = ((), (), s32[]{:S(2)}) async-start(), calls=%async_computation.11 | async-start | bytes 10027008 | tf_op jit(solution)/shard_map/reduce_scatter | solution.py:145
  271.6 277.9 %reduce-scatter.5.cloned.1.call-start = ((), (), s32[]{:S(2)}) async-start(), calls=%async_computation.8 | async-start | bytes 7520256 | tf_op jit(solution)/shard_map/reduce_scatter | solution.py:143
  277.9 49.1 %copy-start.30 = (f32[1024,12]{0,1:T(8,128)S(1)}, f32[1024,12]{0,1:T(8,128)}, u32[]{:S(2)}) copy-start(f32[1024,12]{0,1:T(8,128)} %copy-done.29) | copy-start | bytes 147460
  347.8 22.9 %copy-start.18 = (f32[12,1024,32]{1,2,0:T(8,128)S(1)}, f32[12,1024,32]{1,2,0:T(8,128)}, u32[]{:S(2)}) copy-start(f32[12,1024,32]{1,2,0:T(8,128)} %get-tuple-element.161) | copy-start | bytes 4718596
  374.7 22.9 %copy-start.17 = (f32[12,1024,32]{1,2,0:T(8,128)S(1)}, f32[12,1024,32]{1,2,0:T(8,128)}, u32[]{:S(2)}) copy-start(f32[12,1024,32]{1,2,0:T(8,128)} %get-tuple-element.159) | copy-start | bytes 4718596
  430.2 216.5 %reduce-scatter.9.cloned.1.call-start = ((), (), s32[]{:S(2)}) async-start(), calls=%async_computation.10 | async-start | bytes 10027008 | tf_op jit(solution)/shard_map/reduce_scatter | solution.py:143
  441.6 233.7 %all-reduce.26.cloned.1.call-start = ((), (), s32[]{:S(2)}) async-start(), calls=%async_computation.12 | async-start | bytes 737280 | tf_op jit(solution)/shard_map/psum | solution.py:153
  463.8 12.2 %copy-start.37 = (f32[3072]{0:T(1024)S(1)}, f32[3072]{0:T(1024)}, u32[]{:S(2)}) copy-start(f32[3072]{0:T(1024)} %get-tuple-element.172) | copy-start | bytes 36868
  463.8 12.2 %copy-start.39 = (f32[768]{0:T(1024)S(1)}, f32[768]{0:T(1024)}, u32[]{:S(2)}) copy-start(f32[768]{0:T(1024)} %get-tuple-element.170) | copy-start | bytes 9220
  (34 other events, 96.0 us)
Sparse Core Ops, SparseCore 0:
  10.3 50.8 all-gather.6
  63.5 36.6 all-gather.8
  102.5 52.3 all-gather.10
  157.0 51.7 all-gather.12
  261.3 60.1 reduce-scatter.6
  326.1 110.3 reduce-scatter.10
  440.5 90.3 reduce-scatter.4
  535.6 111.0 reduce-scatter.8
  650.1 25.1 all-reduce.25
